TPU v7x, 32 devices: a whole 2x2x4 slice. The times are simulated.
32 devices in a mesh: band: 8 (over z, y), tok: 4 (over x, core).
Axes of the slice: x: 2, y: 2, z: 4, core: 2. Of those that a mesh axis runs over, the one named last changes fastest.
Arguments:
- pixels: bfloat16 [4, 8, 32, 256, 256], P('tok', None, 'band'), may hold values from -6 to 6
- wave_table: float32 [64], replicated, may hold values from 0.4 to 12
- wave_index: int32 [4, 8, 32], P('tok'), may hold values from 0 to 63
- patch_count: int32 [4, 8], P('tok', 'band'), may hold values from 49 to 256, as said below
- d_out: bfloat16 [4, 8, 256, 768], P('tok', 'band'), may hold values from -6 to 6
- gen_w: bfloat16 [196608, 128], P(('band', 'tok')), may hold values from -0.5 to 0.5
- gen_b: float32 [128, 768], replicated, may hold values from -0.25 to 0.25
- bias_token: float32 [128], replicated, may hold values from -6 to 6
- hyper_query: float32 [128, 128], replicated, may hold values from -1 to 1
- hyper_key: float32 [128, 128], replicated, may hold values from -1 to 1
- hyper_value: float32 [128, 128], replicated, may hold values from -0.5 to 0.5
- hyper_out: float32 [128, 128], replicated, may hold values from -0.5 to 0.5
- hyper_up: float32 [128, 2048], replicated, may hold values from -0.5 to 0.5
- hyper_down: float32 [2048, 128], replicated, may hold values from -0.125 to 0.125
- hyper_gain1: float32 [128], replicated, may hold values from 0.1 to 1.9
- hyper_gain2: float32 [128], replicated, may hold values from 0.1 to 1.9
- w_qkv: bfloat16 [768, 2304], P(None, 'tok'), may hold values from -0.21875 to 0.21875
- w_out: bfloat16 [768, 768], P(None, 'tok'), may hold values from -1.75 to 1.75
- w_up: bfloat16 [768, 3072], P(None, 'tok'), may hold values from -0.21875 to 0.21875
- w_down: bfloat16 [3072, 768], P('tok'), may hold values from -0.109375 to 0.109375
- ln1_gain: float32 [768], replicated, may hold values from 0.5 to 1.5
- ln2_gain: float32 [768], replicated, may hold values from 0.5 to 1.5
Outputs:
- layer_out: bfloat16 [4, 8, 256, 768], P('tok', 'band')
- pixel_grad: bfloat16 [4, 8, 32, 256, 256], P('tok', None, 'band')
- grad_gen_w: float32 [196608, 128], P(('band', 'tok'))
- grad_gen_b: float32 [128, 768], replicated
- grad_bias_token: float32 [128], replicated
- grad_hyper_query: float32 [128, 128], replicated
- grad_hyper_key: float32 [128, 128], replicated
- grad_hyper_value: float32 [128, 128], replicated
- grad_hyper_out: float32 [128, 128], replicated
- grad_hyper_up: float32 [128, 2048], replicated
- grad_hyper_down: float32 [2048, 128], replicated
- grad_hyper_gain1: float32 [128], replicated
- grad_hyper_gain2: float32 [128], replicated
- grad_w_qkv: float32 [768, 2304], P(None, ('band', 'tok'))
- grad_w_out: float32 [768, 768], P(None, ('band', 'tok'))
- grad_w_up: float32 [768, 3072], P(None, ('band', 'tok'))
- grad_w_down: float32 [3072, 768], P(('band', 'tok'))
- grad_ln1_gain: float32 [768], P(('band', 'tok'))
- grad_ln2_gain: float32 [768], P(('band', 'tok'))
Inputs may be any that keep to these rules, and one draw needn't show every extreme that they name: `patch_count`: each entry is 49, 196 or 256; every draw has an image with 49 and one with 256.
All inputs are finite; a program needn't handle non-finite values.
Results may differ from a plain program's by a relative error of at most 0.028.
Values may be sent and summed in bfloat16 or wider, within the bound.
A program may use at most 384 MiB of HBM per device.

v0:
```python
import math
import jax
import jax.numpy as jnp
from jax import lax
from jax.sharding import PartitionSpec as P

HD = 64
HHEADS = 4
EPS_BLOCK = 1e-06
EPS_HYPER = 1e-05
PRECISE = lax.Precision.HIGHEST


def layer_norm(values, scaling, epsilon):
    center = values - jnp.mean(values, axis=-1, keepdims=True)
    spread = jnp.mean(center * center, axis=-1, keepdims=True)
    return center * lax.rsqrt(spread + epsilon) * scaling


def block_norm(values, scaling):
    return layer_norm(values, scaling, EPS_BLOCK)


def exact_gelu(values):
    return jax.nn.gelu(values, approximate=False)


def wave_features(lengths, model_dim):
    middle = model_dim // 2
    angular = 1.0 / 10000.0 ** (jnp.arange(middle, dtype=jnp.float32) / middle)
    phases = (100.0 * lengths)[..., None] * angular
    return jnp.concatenate([jnp.sin(phases), jnp.cos(phases)], axis=-1)


def hyper_layer(features, params):
    (
        bias_token,
        hyper_query,
        hyper_key,
        hyper_value,
        hyper_out,
        hyper_up,
        hyper_down,
        hyper_gain1,
        hyper_gain2,
    ) = params
    images = features.shape[0]
    model_dim = features.shape[-1]
    head_size = model_dim // HHEADS
    tokens = jnp.concatenate(
        [features, jnp.broadcast_to(bias_token, (images, 1, model_dim))], axis=1
    )
    length = tokens.shape[1]
    queries = jnp.einsum("nsc,ce->nse", tokens, hyper_query, precision=PRECISE).reshape(
        images, length, HHEADS, head_size
    )
    keys_all = jnp.einsum("nsc,ce->nse", tokens, hyper_key, precision=PRECISE).reshape(
        images, length, HHEADS, head_size
    )
    values_all = jnp.einsum("nsc,ce->nse", tokens, hyper_value, precision=PRECISE).reshape(
        images, length, HHEADS, head_size
    )
    scores = jnp.einsum("nshe,nthe->nhst", queries, keys_all, precision=PRECISE) / math.sqrt(
        head_size
    )
    weights = jax.nn.softmax(scores, axis=-1)
    blended = jnp.einsum("nhst,nthe->nshe", weights, values_all, precision=PRECISE).reshape(
        images, length, model_dim
    )
    segment_one = layer_norm(
        tokens + jnp.einsum("nse,ef->nsf", blended, hyper_out, precision=PRECISE),
        hyper_gain1,
        EPS_HYPER,
    )
    expanded = jax.nn.gelu(
        jnp.einsum("nse,ef->nsf", segment_one, hyper_up, precision=PRECISE), approximate=False
    )
    second = layer_norm(
        segment_one + jnp.einsum("nsf,fe->nse", expanded, hyper_down, precision=PRECISE),
        hyper_gain2,
        EPS_HYPER,
    )
    return (second[:, :-1, :], second[:, -1, :])


def contract_rows(left_side, right_side):
    return lax.dot_general(
        left_side, right_side, (((0,), (0,)), ((), ())), preferred_element_type=jnp.float32
    )


def contract_cols(left_side, right_side):
    return lax.dot_general(
        left_side, right_side, (((1,), (1,)), ((), ())), preferred_element_type=jnp.float32
    )


def attention_scores(queries, keys_low, usable):
    head_size = queries.shape[-1]
    scores = jnp.einsum(
        "iqhe,ikhe->ihqk", queries, keys_low, preferred_element_type=jnp.float32
    ) / math.sqrt(head_size)
    return jnp.where(usable[:, None, None, :], scores, -1e30)


def block_forward(embedded, usable, weights_full, ln1_gain, ln2_gain):
    w_qkv_full, w_out_full, w_up_full, w_down_full = weights_full
    images, slot_count, model_dim = embedded.shape
    row_count = images * slot_count
    head_count = model_dim // HD
    flat_rows = embedded.reshape(row_count, model_dim)
    normed_one = block_norm(flat_rows, ln1_gain).astype(jnp.bfloat16)
    qkv_low = jnp.dot(normed_one, w_qkv_full, preferred_element_type=jnp.float32).astype(
        jnp.bfloat16
    )
    sections = qkv_low.reshape(images, slot_count, 3, head_count, HD)
    queries = sections[:, :, 0]
    keys_low = sections[:, :, 1]
    values_low = sections[:, :, 2]
    scores = attention_scores(queries, keys_low, usable)
    highest = jnp.max(scores, axis=-1, keepdims=True)
    lifted = jnp.exp(scores - highest)
    totals = jnp.sum(lifted, axis=-1, keepdims=True)
    attn_probs = (lifted / totals).astype(jnp.bfloat16)
    log_mass = highest + jnp.log(totals)
    attended = (
        jnp.einsum("ihqk,ikhe->iqhe", attn_probs, values_low, preferred_element_type=jnp.float32)
        .astype(jnp.bfloat16)
        .reshape(row_count, model_dim)
    )
    middle = flat_rows + jnp.dot(attended, w_out_full, preferred_element_type=jnp.float32)
    normed_two = block_norm(middle, ln2_gain).astype(jnp.bfloat16)
    hidden = jnp.dot(normed_two, w_up_full, preferred_element_type=jnp.float32)
    active = exact_gelu(hidden).astype(jnp.bfloat16)
    output = middle + jnp.dot(active, w_down_full, preferred_element_type=jnp.float32)
    return (
        flat_rows,
        normed_one,
        queries,
        keys_low,
        values_low,
        log_mass,
        attended,
        middle,
        normed_two,
        hidden,
        active,
        output,
    )


def block_backward(stored, usable, grad_rows, weights_full, ln1_gain, ln2_gain):
    (
        flat_rows,
        normed_one,
        queries,
        keys_low,
        values_low,
        log_mass,
        attended,
        middle,
        normed_two,
        hidden,
        active,
        output,
    ) = stored
    w_qkv_full, w_out_full, w_up_full, w_down_full = weights_full
    images, slot_count, head_count, head_size = queries.shape
    row_count, model_dim = flat_rows.shape
    grad_low = grad_rows.astype(jnp.bfloat16)
    grad_down = contract_rows(active, grad_low)
    d_active = contract_cols(grad_low, w_down_full)
    gelu_back = jax.vjp(exact_gelu, hidden)[1]
    d_hidden = gelu_back(d_active)[0].astype(jnp.bfloat16)
    grad_up_turned = contract_rows(d_hidden, normed_two)
    d_normed_two = contract_cols(d_hidden, w_up_full)
    norm_back_two = jax.vjp(block_norm, middle, ln2_gain)[1]
    d_middle_norm, grad_gain_two = norm_back_two(d_normed_two)
    d_middle = grad_rows + d_middle_norm
    d_middle_low = d_middle.astype(jnp.bfloat16)
    grad_out_turned = contract_rows(d_middle_low, attended)
    d_attended = (
        contract_cols(d_middle_low, w_out_full)
        .astype(jnp.bfloat16)
        .reshape(images, slot_count, head_count, head_size)
    )
    scores = attention_scores(queries, keys_low, usable)
    attn_float = jnp.exp(scores - log_mass)
    attn_probs = attn_float.astype(jnp.bfloat16)
    d_values = jnp.einsum(
        "ihqk,iqhe->ikhe", attn_probs, d_attended, preferred_element_type=jnp.float32
    ).astype(jnp.bfloat16)
    d_probs = jnp.einsum(
        "iqhe,ikhe->ihqk", d_attended, values_low, preferred_element_type=jnp.float32
    )
    d_scores = (
        attn_float * (d_probs - jnp.sum(attn_float * d_probs, axis=-1, keepdims=True))
    ).astype(jnp.bfloat16)
    d_queries = (
        jnp.einsum("ihqk,ikhe->iqhe", d_scores, keys_low, preferred_element_type=jnp.float32)
        / math.sqrt(head_size)
    ).astype(jnp.bfloat16)
    d_keys = (
        jnp.einsum("ihqk,iqhe->ikhe", d_scores, queries, preferred_element_type=jnp.float32)
        / math.sqrt(head_size)
    ).astype(jnp.bfloat16)
    d_qkv = jnp.stack([d_queries, d_keys, d_values], axis=2).reshape(row_count, 3 * model_dim)
    grad_qkv_turned = contract_rows(d_qkv, normed_one)
    d_normed_one = contract_cols(d_qkv, w_qkv_full)
    norm_back_one = jax.vjp(block_norm, flat_rows, ln1_gain)[1]
    d_flat, grad_gain_one = norm_back_one(d_normed_one)
    return (
        d_middle + d_flat,
        (grad_qkv_turned, grad_out_turned, grad_up_turned, grad_down, grad_gain_one, grad_gain_two),
    )


def body(
    pixels,
    wave_table,
    wave_index,
    patch_count,
    d_out,
    gen_w,
    gen_b,
    bias_token,
    hyper_query,
    hyper_key,
    hyper_value,
    hyper_out,
    hyper_up,
    hyper_down,
    hyper_gain1,
    hyper_gain2,
    w_qkv,
    w_out,
    w_up,
    w_down,
    ln1_gain,
    ln2_gain,
):
    group_images = pixels.shape[1]
    band_share = pixels.shape[2]
    slot_count = pixels.shape[3]
    pixel_count = pixels.shape[4]
    own_images = patch_count.shape[1]
    model_dim = w_out.shape[0]
    hyper_dim = gen_w.shape[1]
    all_bands = wave_index.shape[2]
    factor = 1.0 / math.sqrt(all_bands * pixel_count)
    band_place = lax.axis_index("band")
    hyper_params = (
        bias_token,
        hyper_query,
        hyper_key,
        hyper_value,
        hyper_out,
        hyper_up,
        hyper_down,
        hyper_gain1,
        hyper_gain2,
    )
    catalog = lax.broadcasted_iota(jnp.int32, (1, 1, wave_table.shape[0]), 2)
    picked = (wave_index[0][:, :, None] == catalog).astype(jnp.float32)
    lengths_all = jnp.sum(picked * wave_table, axis=-1)
    weights_full = (
        lax.all_gather(w_qkv, "tok", axis=1, tiled=True),
        lax.all_gather(w_out, "tok", axis=1, tiled=True),
        lax.all_gather(w_up, "tok", axis=1, tiled=True),
        lax.all_gather(w_down, "tok", axis=0, tiled=True),
    )
    hyper_input = wave_features(lengths_all, hyper_dim)

    def run_hyper(params):
        return hyper_layer(hyper_input, params)

    (band_feats, bias_feats), hyper_back = jax.vjp(run_hyper, hyper_params)
    band_low = (
        lax.dynamic_slice_in_dim(band_feats, band_place * band_share, band_share, 1)
        .astype(jnp.bfloat16)
        .reshape(-1, hyper_dim)
    )
    bias_own = lax.dynamic_slice_in_dim(bias_feats, band_place * own_images, own_images, 0)
    gen_full = lax.all_gather(gen_w, ("band", "tok"), axis=0, tiled=True)
    kernels = (contract_cols(band_low, gen_full) * factor).astype(jnp.bfloat16)
    kernel_grid = kernels.reshape(group_images, band_share, pixel_count, model_dim)
    pixel_part = pixels[0]
    product = jnp.einsum(
        "ibsp,ibpd->isd", pixel_part, kernel_grid, preferred_element_type=jnp.float32
    )
    convolved = lax.psum_scatter(
        product.reshape(own_images * slot_count * lax.axis_size("band"), model_dim).astype(
            jnp.bfloat16
        ),
        "band",
        scatter_dimension=0,
        tiled=True,
    ).astype(jnp.float32)
    bias_rows = jnp.dot(bias_own, gen_b, precision=PRECISE)
    embedded = convolved.reshape(own_images, slot_count, model_dim) + bias_rows[:, None, :]
    usable = lax.broadcasted_iota(jnp.int32, (own_images, slot_count), 1) < patch_count[0][:, None]
    stored = block_forward(embedded, usable, weights_full, ln1_gain, ln2_gain)
    row_mask = usable.reshape(-1, 1)
    layer_out = (
        jnp.where(row_mask, stored[-1], 0.0)
        .astype(jnp.bfloat16)
        .reshape(1, own_images, slot_count, model_dim)
    )
    stored = block_forward(
        lax.optimization_barrier(embedded), usable, weights_full, ln1_gain, ln2_gain
    )
    grad_rows = jnp.where(row_mask, d_out[0].reshape(-1, model_dim).astype(jnp.float32), 0.0)
    d_embed, block_terms = block_backward(
        stored, usable, grad_rows, weights_full, ln1_gain, ln2_gain
    )
    d_embed_low = d_embed.astype(jnp.bfloat16).reshape(own_images, slot_count, model_dim)
    d_bias = jnp.sum(d_embed.reshape(own_images, slot_count, model_dim), axis=1)
    d_bias_feat = jnp.dot(d_bias, gen_b.T, precision=PRECISE)
    grad_gen_b = jnp.dot(bias_own.T, d_bias, precision=PRECISE)
    d_gathered = lax.all_gather(d_embed_low, "band", axis=0, tiled=True)
    pixel_grad = jnp.einsum(
        "isd,ibpd->ibsp", d_gathered, kernel_grid, preferred_element_type=jnp.float32
    ).astype(jnp.bfloat16)[None]
    d_kernel = (
        jnp.einsum("ibsp,isd->ibpd", pixels[0], d_gathered, preferred_element_type=jnp.float32)
        .astype(jnp.bfloat16)
        .reshape(-1, pixel_count * model_dim)
    )
    d_band_local = jnp.dot(d_kernel, gen_full, preferred_element_type=jnp.float32) * factor
    grad_gen_w = lax.psum_scatter(
        contract_rows(d_kernel, band_low) * factor, ("band", "tok"), scatter_dimension=0, tiled=True
    )
    d_band_own = d_band_local.reshape(group_images, band_share, hyper_dim)
    d_band = lax.dynamic_update_slice_in_dim(
        jnp.zeros(band_feats.shape, jnp.float32), d_band_own, band_place * band_share, 1
    )
    d_bias_all = lax.dynamic_update_slice_in_dim(
        jnp.zeros(bias_feats.shape, jnp.float32), d_bias_feat, band_place * own_images, 0
    )
    (
        grad_token,
        grad_query,
        grad_key,
        grad_value,
        grad_mix,
        grad_expand,
        grad_shrink,
        grad_first_gain,
        grad_second_gain,
    ) = hyper_back((d_band, d_bias_all))[0]
    qkv_turned, out_turned, up_turned, grad_down, gain_one, gain_two = block_terms
    block_sums = (
        lax.psum_scatter(qkv_turned, ("band", "tok"), scatter_dimension=0, tiled=True),
        lax.psum_scatter(out_turned, ("band", "tok"), scatter_dimension=0, tiled=True),
        lax.psum_scatter(up_turned, ("band", "tok"), scatter_dimension=0, tiled=True),
        lax.psum_scatter(grad_down, ("band", "tok"), scatter_dimension=0, tiled=True),
        lax.psum_scatter(gain_one, ("band", "tok"), scatter_dimension=0, tiled=True),
        lax.psum_scatter(gain_two, ("band", "tok"), scatter_dimension=0, tiled=True),
    )
    hyper_sums = lax.psum(
        (
            grad_token,
            grad_query,
            grad_key,
            grad_value,
            grad_mix,
            grad_expand,
            grad_shrink,
            grad_first_gain,
            grad_second_gain,
            grad_gen_b,
        ),
        ("band", "tok"),
    )
    return (
        layer_out,
        pixel_grad,
        grad_gen_w,
        hyper_sums[9],
        hyper_sums[0],
        hyper_sums[1],
        hyper_sums[2],
        hyper_sums[3],
        hyper_sums[4],
        hyper_sums[5],
        hyper_sums[6],
        hyper_sums[7],
        hyper_sums[8],
        block_sums[0].T,
        block_sums[1].T,
        block_sums[2].T,
        block_sums[3],
        block_sums[4],
        block_sums[5],
    )


def solution(mesh):
    placed = (
        P("tok", None, "band", None, None),
        P(),
        P("tok", None, None),
        P("tok", "band"),
        P("tok", "band", None, None),
        P(("band", "tok"), None),
        P(),
        P(),
        P(),
        P(),
        P(),
        P(),
        P(),
        P(),
        P(),
        P(),
        P(None, "tok"),
        P(None, "tok"),
        P(None, "tok"),
        P("tok", None),
        P(),
        P(),
    )
    return jax.shard_map(
        body,
        mesh=mesh,
        in_specs=placed,
        out_specs=(
            P("tok", "band", None, None),
            P("tok", None, "band", None, None),
            P(("band", "tok"), None),
            P(),
            P(),
            P(),
            P(),
            P(),
            P(),
            P(),
            P(),
            P(),
            P(),
            P(None, ("band", "tok")),
            P(None, ("band", "tok")),
            P(None, ("band", "tok")),
            P(("band", "tok"), None),
            P(("band", "tok")),
            P(("band", "tok")),
        ),
        check_vma=False,
    )
```

profile of v0, /device:TPU:0, one launch (start us, length us, event | category | flops | bytes accessed | tf_op | source)
XLA Modules:
  0.0 2059.1 jit_solution(18307944858478254983)
XLA Ops:
  21.3 6.0 fusion.22
  30.2 259.9 %all-gather.8.cloned.1.call-done = bf16[196608,128]{1,0:T(8,128)(2,1)} async-done(((bf16[6144,128]{1,0:T(8,128)(2,1)}), bf16[196608,128]{1,0:T(8,128)(2,1)}) %all-gather.8.cloned.1.call-update) | async-done | bytes 50331664 | tf_op jit(solution)/shard_map/all_gather | solution.py:284
  290.0 25.9 %fusion.1 = bf16[32,196608]{1,0:T(8,128)(2,1)} fusion(bf16[32,128]{1,0:T(8,128)(2,1)S(1)} %bitcast.310, bf16[196608,128]{1,0:T(8,128)(2,1)} %all-gather.8.cloned.1.call-done), kind=kOutput, calls=%fused_computation.3 | convolution fusion | flops 1623195648 | bytes 62922752 | tf_op jit(solution)/shard_map/dot_general | solution.py:93
  315.9 8.2 copy.211
  333.5 69.1 %reduce-scatter.7.cloned.1.call-done = bf16[256,768]{1,0:T(8,128)(2,1)} async-done(((bf16[2048,768]{1,0:T(8,128)(2,1)}), bf16[256,768]{1,0:T(8,128)(2,1)}) %reduce-scatter.7.cloned.1.call-update) | async-done | bytes 393232 | tf_op jit(solution)/shard_map/reduce_scatter | solution.py:291
  427.7 29.5 %all-gather.16.cloned.1.call-done = bf16[3072,768]{1,0:T(8,128)(2,1)} async-done(((bf16[768,768]{1,0:T(8,128)(2,1)}), bf16[3072,768]{1,0:T(8,128)(2,1)}) %all-gather.16.cloned.1.call-update) | async-done | bytes 4718608 | tf_op jit(solution)/shard_map/all_gather | solution.py:270
  457.3 10.8 add_convert_fusion
  495.9 51.9 %all-gather.18.cloned.1.call-done = bf16[2048,768]{1,0:T(8,128)(2,1)} async-done(((bf16[256,768]{1,0:T(8,128)(2,1)}), bf16[2048,768]{1,0:T(8,128)(2,1)}) %all-gather.18.cloned.1.call-update) | async-done | bytes 3145744 | tf_op jit(solution)/shard_map/all_gather | solution.py:320
  547.8 11.1 convert_bitcast_fusion
  558.8 16.8 copy.212
  575.6 23.0 %convolution_multiply_fusion.5 = f32[32,128]{1,0:T(8,128)S(1)} fusion(bf16[32,196608]{1,0:T(8,128)(2,1)} %bitcast.272, bf16[196608,128]{1,0:T(8,128)(2,1)} %all-gather.8.cloned.1.call-done), kind=kOutput, calls=%fused_computation.123 | convolution fusion | flops 1610616832 | bytes 62930944 | tf_op jit(solution)/shard_map/dot_general | solution.py:329
  628.8 6.3 convolution_bitcast_fusion
  641.6 11.6 fusion.34
  653.9 6.6 fusion.194
  661.3 39.6 %convolution_multiply_fusion = f32[196608,128]{1,0:T(8,128)} fusion(bf16[32,196608]{1,0:T(8,128)(2,1)} %bitcast.273, bf16[32,128]{1,0:T(8,128)(2,1)S(1)} %bitcast.311), kind=kOutput, calls=%fused_computation.1 | convolution fusion | flops 1635778560 | bytes 113254400 | tf_op jit(solution)/shard_map/dot_general | solution.py:87
  710.2 13.5 fusion.65
  723.7 11.1 convert_bitcast_fusion.1
  734.9 6.6 copy.179
  745.3 39.6 %all-reduce.4 = (f32[128]{0:T(128)}, f32[128]{0:T(128)}, f32[128]{0:T(128)}, f32[768]{0:T(1024)S(1)}, f32[768]{0:T(1024)S(1)}) all-reduce(f32[128]{0:T(128)S(1)} %fusion.148, f32[128]{0:T(128)S(1)} %copy-done.107, f32[128]{0:T(128)S(1)} %copy-done.106, f32[768]{0:T(1024)S(1)} %copy-done.105, ...), channel_id=1, replica_groups=mesh['band'=8,'tok'=4] {'band','tok'}, use_global_device_ids=true, to_apply=%region_34.35 | all-reduce | flops 1920 | bytes 15360 | tf_op jit(solution)/shard_map/psum | solution.py:360
  786.1 12.8 all-reduce.8.cloned.1.call-done
  798.9 124.6 %reduce-scatter.11.cloned.1.call-done = f32[72,768]{1,0:T(8,128)} async-done(((f32[2304,768]{1,0:T(8,128)}), f32[72,768]{1,0:T(8,128)}) %reduce-scatter.11.cloned.1.call-update) | async-done | bytes 221200 | tf_op jit(solution)/shard_map/reduce_scatter | solution.py:353
  923.5 142.3 %reduce-scatter.17.cloned.1.call-done = f32[96,768]{1,0:T(8,128)} async-done(((f32[3072,768]{1,0:T(8,128)}), f32[96,768]{1,0:T(8,128)}) %reduce-scatter.17.cloned.1.call-update) | async-done | bytes 294928 | tf_op jit(solution)/shard_map/reduce_scatter | solution.py:356
  1065.8 141.0 %reduce-scatter.15.cloned.1.call-done = f32[96,768]{1,0:T(8,128)} async-done(((f32[3072,768]{1,0:T(8,128)}), f32[96,768]{1,0:T(8,128)}) %reduce-scatter.15.cloned.1.call-update) | async-done | bytes 294928 | tf_op jit(solution)/shard_map/reduce_scatter | solution.py:355
  1206.8 833.8 %reduce-scatter.9.cloned.1.call-done = f32[6144,128]{1,0:T(8,128)} async-done(((f32[196608,128]{1,0:T(8,128)}), f32[6144,128]{1,0:T(8,128)}) %reduce-scatter.9.cloned.1.call-update) | async-done | bytes 3145744 | tf_op jit(solution)/shard_map/reduce_scatter | solution.py:330
  (373 shorter events, 139.6 us)
Async XLA Ops:
  8.1 282.0 %all-gather.8.cloned.1.call-start = ((), (), s32[]{:S(2)}) async-start(), calls=%async_computation.6 | async-start | bytes 51904512 | tf_op jit(solution)/shard_map/all_gather | solution.py:284
  8.8 393.8 %reduce-scatter.7.cloned.1.call-start = ((), (), s32[]{:S(2)}) async-start(), calls=%async_computation.7 | async-start | bytes 3538944 | tf_op jit(solution)/shard_map/reduce_scatter | solution.py:291
  29.9 286.0 %copy-start.67 = (f32[8,33]{1,0:T(8,128)}, f32[8,33]{1,0:T(8,128)S(1)}, u32[]{:S(2)}) copy-start(f32[8,33]{1,0:T(8,128)S(1)} %multiply_reduce_fusion.14) | copy-start | bytes 3172
  30.2 285.8 %copy-start.57 = (bf16[8,4,128]{2,1,0:T(4,128)(2,1)}, bf16[8,4,128]{2,1,0:T(4,128)(2,1)S(1)}, u32[]{:S(2)}) copy-start(bf16[8,4,128]{2,1,0:T(4,128)(2,1)S(1)} %dynamic-slice_convert_fusion) | copy-start | bytes 24580
  329.9 76.1 %all-gather.10.cloned.1.call-start = ((), (), s32[]{:S(2)}) async-start(), calls=%async_computation.8 | async-start | bytes 4423680 | tf_op jit(solution)/shard_map/all_gather | solution.py:267
  330.5 75.6 %copy-start.69 = (f32[768]{0:T(1024)S(1)}, f32[768]{0:T(1024)}, u32[]{:S(2)}) copy-start(f32[768]{0:T(1024)} %param.42) | copy-start | bytes 9220
  330.5 88.0 %all-gather.12.cloned.1.call-start = ((), (), s32[]{:S(2)}) async-start(), calls=%async_computation.9 | async-start | bytes 1474560 | tf_op jit(solution)/shard_map/all_gather | solution.py:268
  331.1 91.2 %all-gather.14.cloned.1.call-start = ((), (), s32[]{:S(2)}) async-start(), calls=%async_computation.10 | async-start | bytes 5898240 | tf_op jit(solution)/shard_map/all_gather | solution.py:269
  331.6 125.6 %all-gather.16.cloned.1.call-start = ((), (), s32[]{:S(2)}) async-start(), calls=%async_computation.11 | async-start | bytes 5898240 | tf_op jit(solution)/shard_map/all_gather | solution.py:270
  332.4 215.4 %all-gather.18.cloned.1.call-start = ((), (), s32[]{:S(2)}) async-start(), calls=%async_computation.17 | async-start | bytes 3538944 | tf_op jit(solution)/shard_map/all_gather | solution.py:320
  332.4 73.2 %copy-start.94 = (f32[8,1,128]{2,1,0:T(1,128)}, f32[8,1,128]{2,1,0:T(1,128)S(1)}, u32[]{:S(2)}) copy-start(f32[8,1,128]{2,1,0:T(1,128)S(1)} %slice.33) | copy-start | bytes 12292
  333.1 80.0 %copy-start.95 = (pred[256]{0:T(512)(128)(4,1)}, pred[256]{0:T(512)(128)(4,1)S(1)}, u32[]{:S(2)}) copy-start(pred[256]{0:T(512)(128)(4,1)S(1)} %iota_compare_fusion.1) | copy-start | bytes 772
  333.5 76.8 %copy-start.59 = (f32[768]{0:T(1024)}, f32[768]{0:T(1024)S(1)}, u32[]{:S(2)}) copy-start(f32[768]{0:T(1024)S(1)} %convolution_reduce_fusion) | copy-start | bytes 9220
  487.1 299.0 %reduce-scatter.13.cloned.1.call-start = ((), (), s32[]{:S(2)}) async-start(), calls=%async_computation.14 | async-start | bytes 2433024 | tf_op jit(solution)/shard_map/reduce_scatter | solution.py:354
  494.3 304.5 %all-reduce.8.cloned.1.call-start = ((), (), s32[]{:S(2)}) async-start(), calls=%async_computation.18 | async-start | bytes 5505024 | tf_op jit(solution)/shard_map/psum | solution.py:360
  575.6 23.8 %copy-start.68 = (f32[8,33]{1,0:T(8,128)S(1)}, f32[8,33]{1,0:T(8,128)}, u32[]{:S(2)}) copy-start(f32[8,33]{1,0:T(8,128)} %copy-done.67) | copy-start | bytes 3172
  575.6 24.1 %copy-start.5 = (f32[8,33,2048]{2,1,0:T(8,128)S(1)}, f32[8,33,2048]{2,1,0:T(8,128)}, u32[]{:S(2)}) copy-start(f32[8,33,2048]{2,1,0:T(8,128)} %copy-done.4) | copy-start | bytes 6488068
  575.6 24.1 %copy-start.8 = (f32[8,33,2048]{2,1,0:T(8,128)S(1)}, f32[8,33,2048]{2,1,0:T(8,128)}, u32[]{:S(2)}) copy-start(f32[8,33,2048]{2,1,0:T(8,128)} %copy-done.7) | copy-start | bytes 6488068
  635.1 288.3 %reduce-scatter.11.cloned.1.call-start = ((), (), s32[]{:S(2)}) async-start(), calls=%async_computation.13 | async-start | bytes 7299072 | tf_op jit(solution)/shard_map/reduce_scatter | solution.py:353
  640.6 425.2 %reduce-scatter.17.cloned.1.call-start = ((), (), s32[]{:S(2)}) async-start(), calls=%async_computation.16 | async-start | bytes 9732096 | tf_op jit(solution)/shard_map/reduce_scatter | solution.py:356
  653.2 553.6 %reduce-scatter.15.cloned.1.call-start = ((), (), s32[]{:S(2)}) async-start(), calls=%async_computation.15 | async-start | bytes 9732096 | tf_op jit(solution)/shard_map/reduce_scatter | solution.py:355
  660.6 1380.0 %reduce-scatter.9.cloned.1.call-start = ((), (), s32[]{:S(2)}) async-start(), calls=%async_computation.12 | async-start | bytes 103809024 | tf_op jit(solution)/shard_map/reduce_scatter | solution.py:330
  742.5 1309.1 %copy-start.1 = (f32[128,2048]{1,0:T(8,128)S(1)}, f32[128,2048]{1,0:T(8,128)}, u32[]{:S(2)}) copy-start(f32[128,2048]{1,0:T(8,128)} %param.34) | copy-start | bytes 3145732
  798.9 1251.7 %copy-start.46 = (f32[2048,128]{1,0:T(8,128)S(1)}, f32[2048,128]{1,0:T(8,128)}, u32[]{:S(2)}) copy-start(f32[2048,128]{1,0:T(8,128)} %get-tuple-element.165) | copy-start | bytes 3145732
  (99 other events, 464.0 us)
Sparse Core Ops, SparseCore 0:
  11.8 278.2 all-gather.7
  330.0 72.5 reduce-scatter.6
  487.3 60.4 all-gather.17
  553.5 97.6 reduce-scatter.12
  659.7 139.0 all-reduce.7
  805.0 118.4 reduce-scatter.10
  931.0 134.7 reduce-scatter.16
  1072.3 134.5 reduce-scatter.14
  1215.0 825.6 reduce-scatter.8
Sparse Core Ops, SparseCore 1:
  331.9 28.7 all-gather.9
  362.2 17.3 all-gather.11
  381.0 37.3 all-gather.13
  419.9 37.3 all-gather.15
where the time goes:
time: 2070 us; the launch traced here: 2060 us
  waiting for transfers between devices  1670 us (81%)
  matrix products  245 us (12%)
  local copies, waits for them, and re-layouts  65.3 us (3%)
  blocking collectives  39.6 us (2%)
  other arithmetic  22.8 us (1%)
    reduce_scatter x1, waiting for transfers between devices, body(): lax.psum_scatter(contract_rows(d_kernel, band_low) * factor, ('band', 'to...  834 us
    all_gather x1, waiting for transfers between devices, body(): gen_full = lax.all_gather(gen_w, ('band', 'tok'), axis=0, tiled=True)  260 us
    reduce_scatter x1, waiting for transfers between devices, body(): lax.psum_scatter(grad_down, ('band', 'tok'), scatter_dimension=0, tiled=T...  142 us
    reduce_scatter x1, waiting for transfers between devices, body(): lax.psum_scatter(up_turned, ('band', 'tok'), scatter_dimension=0, tiled=T...  141 us
    reduce_scatter x1, waiting for transfers between devices, body(): lax.psum_scatter(qkv_turned, ('band', 'tok'), scatter_dimension=0, tiled=...  125 us
    reduce_scatter x1, waiting for transfers between devices, body(): lax.psum_scatter(product.reshape(own_images * slot_count * lax.axis_size(...  69.1 us
    dot_general x5, matrix products, contract_rows(): lax.dot_general(left_side, right_side, (((0,), (0,)), ((), ())), preferre...  66.2 us
    unnamed x232, local copies, waits for them, and re-layouts  54.6 us
  transfers between devices with their start and end apart: 13, of which 9 were waited for; matrix products, arithmetic and copies ran while one was open for 12% of the time, Pallas kernels for 0%

commit v1 on v0

--- a/solution.py
+++ b/solution.py
@@ -358,19 +358,22 @@
         lax.psum_scatter(gain_two, ("band", "tok"), scatter_dimension=0, tiled=True),
     )
     hyper_sums = lax.psum(
-        (
-            grad_token,
-            grad_query,
-            grad_key,
-            grad_value,
-            grad_mix,
-            grad_expand,
-            grad_shrink,
-            grad_first_gain,
-            grad_second_gain,
-            grad_gen_b,
+        lax.psum(
+            (
+                grad_token,
+                grad_query,
+                grad_key,
+                grad_value,
+                grad_mix,
+                grad_expand,
+                grad_shrink,
+                grad_first_gain,
+                grad_second_gain,
+                grad_gen_b,
+            ),
+            "tok",
         ),
-        ("band", "tok"),
+        "band",
     )
     return (
         layer_out,

time: 2070 us -> 2140 us (1.034)
  waiting for transfers between devices: 1670 us -> 1710 us
  blocking collectives: 39.6 us -> 67 us
    reduce_scatter x1, waiting for transfers between devices: 125 us -> 0.01 us  [body(): lax.psum_scatter(qkv_turned, ('band', 'tok'), scatter_dimension=0, tiled=...]
    psum x0 -> x1, waiting for transfers between devices: none -> 123 us  [body(): lax.psum(lax.psum((grad_token, grad_query, grad_key, grad_value, grad_mix...]
    psum x1, waiting for transfers between devices: 12.8 us -> 58.2 us  [body(): lax.psum((grad_token, grad_query, grad_key, grad_value, grad_mix, grad_ex...]
    unnamed x0 -> x1, blocking collectives: none -> 39.5 us
    psum x1, blocking collectives: 39.6 us -> 7.06 us  [body(): lax.psum((grad_token, grad_query, grad_key, grad_value, grad_mix, grad_ex...]
    unnamed x232 -> x222, local copies, waits for them, and re-layouts: 54.6 us -> 51.5 us
  transfers between devices with their start and end apart: 13 -> 14, of which waited for: 9 -> 9; matrix products, arithmetic and copies ran while one was open for 12% -> 7% of each run, Pallas kernels for 0% -> 0%
where the time goes in v1:
time: 2140 us; the launch traced here: 2130 us
  waiting for transfers between devices  1710 us (80%)
  matrix products  242 us (11%)
  blocking collectives  67 us (3%)
  local copies, waits for them, and re-layouts  63.3 us (3%)
  other arithmetic  24 us (1%)
    reduce_scatter x1, waiting for transfers between devices, body(): lax.psum_scatter(contract_rows(d_kernel, band_low) * factor, ('band', 'to...  833 us
    all_gather x1, waiting for transfers between devices, body(): gen_full = lax.all_gather(gen_w, ('band', 'tok'), axis=0, tiled=True)  260 us
    reduce_scatter x1, waiting for transfers between devices, body(): lax.psum_scatter(up_turned, ('band', 'tok'), scatter_dimension=0, tiled=T...  142 us
    reduce_scatter x1, waiting for transfers between devices, body(): lax.psum_scatter(grad_down, ('band', 'tok'), scatter_dimension=0, tiled=T...  141 us
    psum x1, waiting for transfers between devices, body(): lax.psum(lax.psum((grad_token, grad_query, grad_key, grad_value, grad_mix...  123 us
    reduce_scatter x1, waiting for transfers between devices, body(): lax.psum_scatter(product.reshape(own_images * slot_count * lax.axis_size(...  69.1 us
    dot_general x5, matrix products, contract_rows(): lax.dot_general(left_side, right_side, (((0,), (0,)), ((), ())), preferre...  65.1 us
    psum x1, waiting for transfers between devices, body(): lax.psum((grad_token, grad_query, grad_key, grad_value, grad_mix, grad_ex...  58.2 us
  transfers between devices with their start and end apart: 14, of which 9 were waited for; matrix products, arithmetic and copies ran while one was open for 7% of the time, Pallas kernels for 0%

profile of v1, /device:TPU:0, one launch (start us, length us, event | category | flops | bytes accessed | tf_op | source)
XLA Modules:
  0.0 2129.2 jit_solution(15623021923495774067)
XLA Ops:
  30.0 260.0 %all-gather.8.cloned.1.call-done = bf16[196608,128]{1,0:T(8,128)(2,1)} async-done(((bf16[6144,128]{1,0:T(8,128)(2,1)}), bf16[196608,128]{1,0:T(8,128)(2,1)}) %all-gather.8.cloned.1.call-update) | async-done | bytes 50331664 | tf_op jit(solution)/shard_map/all_gather | solution.py:284
  290.0 25.8 %fusion.1 = bf16[32,196608]{1,0:T(8,128)(2,1)} fusion(bf16[32,128]{1,0:T(8,128)(2,1)S(1)} %bitcast.310, bf16[196608,128]{1,0:T(8,128)(2,1)} %all-gather.8.cloned.1.call-done), kind=kOutput, calls=%fused_computation.3 | convolution fusion | flops 1623195648 | bytes 62922752 | tf_op jit(solution)/shard_map/dot_general | solution.py:93
  315.9 8.2 copy.211
  333.4 69.1 %reduce-scatter.7.cloned.1.call-done = bf16[256,768]{1,0:T(8,128)(2,1)} async-done(((bf16[2048,768]{1,0:T(8,128)(2,1)}), bf16[256,768]{1,0:T(8,128)(2,1)}) %reduce-scatter.7.cloned.1.call-update) | async-done | bytes 393232 | tf_op jit(solution)/shard_map/reduce_scatter | solution.py:291
  427.2 30.0 %all-gather.16.cloned.1.call-done = bf16[3072,768]{1,0:T(8,128)(2,1)} async-done(((bf16[768,768]{1,0:T(8,128)(2,1)}), bf16[3072,768]{1,0:T(8,128)(2,1)}) %all-gather.16.cloned.1.call-update) | async-done | bytes 4718608 | tf_op jit(solution)/shard_map/all_gather | solution.py:270
  457.2 11.0 add_convert_fusion
  493.5 54.4 %all-gather.18.cloned.1.call-done = bf16[2048,768]{1,0:T(8,128)(2,1)} async-done(((bf16[256,768]{1,0:T(8,128)(2,1)}), bf16[2048,768]{1,0:T(8,128)(2,1)}) %all-gather.18.cloned.1.call-update) | async-done | bytes 3145744 | tf_op jit(solution)/shard_map/all_gather | solution.py:320
  547.9 11.1 convert_bitcast_fusion
  559.0 16.7 copy.212
  575.7 22.2 %convolution_multiply_fusion.5 = f32[32,128]{1,0:T(8,128)S(1)} fusion(bf16[32,196608]{1,0:T(8,128)(2,1)} %bitcast.272, bf16[196608,128]{1,0:T(8,128)(2,1)} %all-gather.8.cloned.1.call-done), kind=kOutput, calls=%fused_computation.123 | convolution fusion | flops 1610616832 | bytes 62930944 | tf_op jit(solution)/shard_map/dot_general | solution.py:329
  641.9 58.2 %all-reduce.14.cloned.1.call-done = (f32[128,768]{1,0:T(8,128)}, f32[128,128]{1,0:T(8,128)}, f32[128,128]{1,0:T(8,128)}, f32[128,128]{1,0:T(8,128)}, f32[128,128...) async-done(((f32[128,768]{1,0:T(8,128)}, f32[128,128]{1,0:T(8,128)}, f32[128,128]{1,0:T(8,128)}, f32[128,128]{1,0:T(8,128)}, f32[128,128]{1,0:T(8,128)}, ...) | async-done | bytes 2752528 | tf_op jit(solution)/shard_map/psum | solution.py:361
  700.2 11.6 fusion.34
  712.5 6.8 fusion.194
  720.0 39.4 %convolution_multiply_fusion = f32[196608,128]{1,0:T(8,128)} fusion(bf16[32,196608]{1,0:T(8,128)(2,1)} %bitcast.273, bf16[32,128]{1,0:T(8,128)(2,1)S(1)} %bitcast.311), kind=kOutput, calls=%fused_computation.1 | convolution fusion | flops 1635778560 | bytes 113254400 | tf_op jit(solution)/shard_map/dot_general | solution.py:87
  764.3 39.5 %all-reduce.4 = (f32[768]{0:T(1024)S(1)}, f32[768]{0:T(1024)S(1)}) all-reduce(f32[768]{0:T(1024)S(1)} %copy-done.100, f32[768]{0:T(1024)S(1)} %copy-done.99), channel_id=9, replica_groups=mesh['band'=8,'tok'=4] {'band','tok'}, use_global_device_ids=true, to_apply=%region_60.61.clone | all-reduce | flops 1536 | bytes 12288
  809.1 13.5 fusion.65
  822.6 11.3 convert_bitcast_fusion.1
  834.0 6.6 copy.179
  844.3 7.1 all-reduce.7
  851.4 20.5 all-reduce.5
  871.8 122.8 %all-reduce.12.cloned.1.call-done = (f32[128,768]{1,0:T(8,128)}, f32[128,128]{1,0:T(8,128)}, f32[128,128]{1,0:T(8,128)}, f32[128,128]{1,0:T(8,128)}, f32[128,128...) async-done(((f32[128,768]{1,0:T(8,128)}, f32[128,128]{1,0:T(8,128)}, f32[128,128]{1,0:T(8,128)}, f32[128,128]{1,0:T(8,128)}, f32[128,128]{1,0:T(8,128)}, ...) | async-done | bytes 2752528 | tf_op jit(solution)/shard_map/psum | solution.py:360
  994.6 140.8 %reduce-scatter.17.cloned.1.call-done = f32[96,768]{1,0:T(8,128)} async-done(((f32[3072,768]{1,0:T(8,128)}), f32[96,768]{1,0:T(8,128)}) %reduce-scatter.17.cloned.1.call-update) | async-done | bytes 294928 | tf_op jit(solution)/shard_map/reduce_scatter | solution.py:356
  1135.4 142.3 %reduce-scatter.15.cloned.1.call-done = f32[96,768]{1,0:T(8,128)} async-done(((f32[3072,768]{1,0:T(8,128)}), f32[96,768]{1,0:T(8,128)}) %reduce-scatter.15.cloned.1.call-update) | async-done | bytes 294928 | tf_op jit(solution)/shard_map/reduce_scatter | solution.py:355
  1277.7 832.7 %reduce-scatter.9.cloned.1.call-done = f32[6144,128]{1,0:T(8,128)} async-done(((f32[196608,128]{1,0:T(8,128)}), f32[6144,128]{1,0:T(8,128)}) %reduce-scatter.9.cloned.1.call-update) | async-done | bytes 3145744 | tf_op jit(solution)/shard_map/reduce_scatter | solution.py:330
  (368 shorter events, 149.6 us)
Async XLA Ops:
  8.1 282.0 %all-gather.8.cloned.1.call-start = ((), (), s32[]{:S(2)}) async-start(), calls=%async_computation.6 | async-start | bytes 51904512 | tf_op jit(solution)/shard_map/all_gather | solution.py:284
  8.8 393.7 %reduce-scatter.7.cloned.1.call-start = ((), (), s32[]{:S(2)}) async-start(), calls=%async_computation.7 | async-start | bytes 3538944 | tf_op jit(solution)/shard_map/reduce_scatter | solution.py:291
  29.8 286.1 %copy-start.63 = (f32[8,33]{1,0:T(8,128)}, f32[8,33]{1,0:T(8,128)S(1)}, u32[]{:S(2)}) copy-start(f32[8,33]{1,0:T(8,128)S(1)} %multiply_reduce_fusion.14) | copy-start | bytes 3172
  30.0 285.8 %copy-start.53 = (bf16[8,4,128]{2,1,0:T(4,128)(2,1)}, bf16[8,4,128]{2,1,0:T(4,128)(2,1)S(1)}, u32[]{:S(2)}) copy-start(bf16[8,4,128]{2,1,0:T(4,128)(2,1)S(1)} %dynamic-slice_convert_fusion) | copy-start | bytes 24580
  329.8 76.0 %all-gather.10.cloned.1.call-start = ((), (), s32[]{:S(2)}) async-start(), calls=%async_computation.8 | async-start | bytes 4423680 | tf_op jit(solution)/shard_map/all_gather | solution.py:267
  330.4 75.5 %copy-start.65 = (f32[768]{0:T(1024)S(1)}, f32[768]{0:T(1024)}, u32[]{:S(2)}) copy-start(f32[768]{0:T(1024)} %param.42) | copy-start | bytes 9220
  330.4 87.6 %all-gather.12.cloned.1.call-start = ((), (), s32[]{:S(2)}) async-start(), calls=%async_computation.9 | async-start | bytes 1474560 | tf_op jit(solution)/shard_map/all_gather | solution.py:268
  331.0 90.7 %all-gather.14.cloned.1.call-start = ((), (), s32[]{:S(2)}) async-start(), calls=%async_computation.10 | async-start | bytes 5898240 | tf_op jit(solution)/shard_map/all_gather | solution.py:269
  331.6 125.6 %all-gather.16.cloned.1.call-start = ((), (), s32[]{:S(2)}) async-start(), calls=%async_computation.11 | async-start | bytes 5898240 | tf_op jit(solution)/shard_map/all_gather | solution.py:270
  332.3 215.6 %all-gather.18.cloned.1.call-start = ((), (), s32[]{:S(2)}) async-start(), calls=%async_computation.17 | async-start | bytes 3538944 | tf_op jit(solution)/shard_map/all_gather | solution.py:320
  332.4 73.1 %copy-start.89 = (f32[8,1,128]{2,1,0:T(1,128)}, f32[8,1,128]{2,1,0:T(1,128)S(1)}, u32[]{:S(2)}) copy-start(f32[8,1,128]{2,1,0:T(1,128)S(1)} %slice.33) | copy-start | bytes 12292
  333.1 79.6 %copy-start.90 = (pred[256]{0:T(512)(128)(4,1)}, pred[256]{0:T(512)(128)(4,1)S(1)}, u32[]{:S(2)}) copy-start(pred[256]{0:T(512)(128)(4,1)S(1)} %iota_compare_fusion.1) | copy-start | bytes 772
  333.4 76.7 %copy-start.55 = (f32[768]{0:T(1024)}, f32[768]{0:T(1024)S(1)}, u32[]{:S(2)}) copy-start(f32[768]{0:T(1024)S(1)} %convolution_reduce_fusion) | copy-start | bytes 9220
  487.3 212.8 %all-reduce.14.cloned.1.call-start = ((), (), s32[]{:S(2)}) async-start(), calls=%async_computation.19 | async-start | bytes 5505024 | tf_op jit(solution)/shard_map/psum | solution.py:361
  634.2 237.6 %reduce-scatter.13.cloned.1.call-start = ((), (), s32[]{:S(2)}) async-start(), calls=%async_computation.14 | async-start | bytes 2433024 | tf_op jit(solution)/shard_map/reduce_scatter | solution.py:354
  636.2 235.6 %reduce-scatter.11.cloned.1.call-start = ((), (), s32[]{:S(2)}) async-start(), calls=%async_computation.13 | async-start | bytes 7299072 | tf_op jit(solution)/shard_map/reduce_scatter | solution.py:353
  641.8 58.3 %copy-start.39 = (bf16[1,1,256,768]{3,2,1,0:T(8,128)(2,1)S(1)}, bf16[1,1,256,768]{3,2,1,0:T(8,128)(2,1)}, u32[]{:S(2)}) copy-start(bf16[1,1,256,768]{3,2,1,0:T(8,128)(2,1)} %param.26) | copy-start | bytes 1179652
  641.8 58.3 %copy-start.93 = (pred[256]{0:T(512)(128)(4,1)S(1)}, pred[256]{0:T(512)(128)(4,1)}, u32[]{:S(2)}) copy-start(pred[256]{0:T(512)(128)(4,1)} %copy-done.90) | copy-start | bytes 772
  641.9 352.7 %all-reduce.12.cloned.1.call-start = ((), (), s32[]{:S(2)}) async-start(), calls=%async_computation.18 | async-start | bytes 5505024 | tf_op jit(solution)/shard_map/psum | solution.py:360
  700.1 435.3 %reduce-scatter.17.cloned.1.call-start = ((), (), s32[]{:S(2)}) async-start(), calls=%async_computation.16 | async-start | bytes 9732096 | tf_op jit(solution)/shard_map/reduce_scatter | solution.py:356
  711.8 565.9 %reduce-scatter.15.cloned.1.call-start = ((), (), s32[]{:S(2)}) async-start(), calls=%async_computation.15 | async-start | bytes 9732096 | tf_op jit(solution)/shard_map/reduce_scatter | solution.py:355
  719.3 1391.1 %reduce-scatter.9.cloned.1.call-start = ((), (), s32[]{:S(2)}) async-start(), calls=%async_computation.12 | async-start | bytes 103809024 | tf_op jit(solution)/shard_map/reduce_scatter | solution.py:330
  841.5 1279.8 %copy-start.1 = (f32[128,2048]{1,0:T(8,128)S(1)}, f32[128,2048]{1,0:T(8,128)}, u32[]{:S(2)}) copy-start(f32[128,2048]{1,0:T(8,128)} %param.34) | copy-start | bytes 3145732
  994.6 1125.8 %copy-start.41 = (f32[2048,128]{1,0:T(8,128)S(1)}, f32[2048,128]{1,0:T(8,128)}, u32[]{:S(2)}) copy-start(f32[2048,128]{1,0:T(8,128)} %get-tuple-element.175) | copy-start | bytes 3145732
  (95 other events, 487.3 us)
Sparse Core Ops, SparseCore 0:
  11.8 278.2 all-gather.7
  330.0 72.5 reduce-scatter.6
  487.4 60.4 all-gather.17
  640.6 103.6 reduce-scatter.12
  751.4 117.9 reduce-scatter.10
  873.8 120.7 all-reduce.11
  1001.1 134.3 reduce-scatter.16
  1142.9 134.7 reduce-scatter.14
  1284.7 825.6 reduce-scatter.8
Sparse Core Ops, SparseCore 1:
  331.9 28.7 all-gather.9
  362.1 17.3 all-gather.11
  380.9 37.3 all-gather.13
  419.9 37.3 all-gather.15
  634.3 65.8 all-reduce.13
